TPU v7x, 32 devices: a whole 2x2x4 slice. The times are simulated.
32 devices in a mesh: grp: 2 (over y), keys: 4 (over x, core), qry: 4 (over z).
Axes of the slice: x: 2, y: 2, z: 4, core: 2. Of those that a mesh axis runs over, the one named last changes fastest.
Arguments:
- queries: bfloat16 [4096, 8, 128], P(('grp', 'keys', 'qry')), parts along dimension 0, may hold values from -40 to 40, as said below
- cache_keys: bfloat16 [4096, 128], P(('grp', 'keys')), parts along dimension 0, may hold values from -128 to 128, as said below
- cache_values: bfloat16 [4096, 128], P(('grp', 'keys')), parts along dimension 0, may hold values from -24 to 24
- entry: int32 [8, 4], P(('grp', 'keys'), 'qry'), parts along dimension 0, may hold values from 0 to 3
- visits: int32 [8, 4], P(('grp', 'keys'), 'qry'), parts along dimension 0, may hold values from 3 to 4
- doc_length: int32 [2], P('grp'), parts along dimension 0, may hold values from 1025 to 2048
- slot_params: float32 [2048, 256], P(('grp', 'keys', 'qry')), parts along dimension 0, may hold values from -128 to 128, as said below
- first_moment: float32 [2048, 256], P(('grp', 'keys', 'qry')), parts along dimension 0, may hold values from -3 to 3
- second_moment: float32 [2048, 256], P(('grp', 'keys', 'qry')), parts along dimension 0, may hold values from 0.05 to 1
Outputs:
- teacher_out: bfloat16 [4096, 8, 128], P(('grp', 'keys', 'qry')), parts along dimension 0
- slot_grad: float32 [2048, 256], P(('grp', 'keys', 'qry')), parts along dimension 0
- new_params: float32 [2048, 256], P(('grp', 'keys', 'qry')), parts along dimension 0
- new_first: float32 [2048, 256], P(('grp', 'keys', 'qry')), parts along dimension 0
- new_second: float32 [2048, 256], P(('grp', 'keys', 'qry')), parts along dimension 0
- loss: float32 [2], P('grp'), parts along dimension 0
There are 2 independent parts, one for each index of `grp`. A program takes and returns all parts, laid end to end along the dimension named above; each array names one. Nothing has to cross between parts.
Inputs may be any that keep to these rules, and one draw needn't show every extreme that they name: `queries`: query entries stay within the stated range. `cache_keys`: cache key entries stay within the stated range. `slot_params`: slot entries stay within the stated range.
All inputs are finite; a program needn't handle non-finite values.
Results may differ from a plain program's by a relative error of at most 0.0045.
Values may be sent and summed in bfloat16 or wider, within the bound.
No kernel may reach another device: no remote copies, remote signals or barrier semaphores. Data moves between devices by JAX's collectives and lax.ppermute only.
A program may use at most 64 MiB of HBM per device.

v0:
```python
import math
import jax
import jax.numpy as jnp
from jax import lax
from jax.sharding import PartitionSpec as P

NEG = -1e30


def shifted(block, axis, distance):
    devices = range(lax.axis_size(axis))
    route = [((i - distance) % len(devices), i) for i in devices]
    return lax.ppermute(block, axis, route)


def row_scores(left, right):
    return lax.dot_general(
        left, right, (((1,), (1,)), ((), ())), preferred_element_type=jnp.float32
    )


def attend(state, query_blocks, keys, values, shard, length, score_scale):
    block_width = keys.shape[0]
    place = shard * block_width + lax.iota(jnp.int32, block_width)
    live = (place < length)[None, :]

    def one(block_entry):
        query_portion, big, total, acc = block_entry
        logit_score = jnp.where(live, row_scores(query_portion, keys) * score_scale, NEG)
        new_big = jnp.maximum(big, jnp.max(logit_score, axis=1))
        weight = jnp.where(live, jnp.exp(logit_score - new_big[:, None]), 0.0)
        fade = jnp.exp(big - new_big)
        total = total * fade + jnp.sum(weight, axis=1)
        acc = acc * fade[:, None] + jnp.dot(
            weight.astype(jnp.bfloat16), values, preferred_element_type=jnp.float32
        )
        return (new_big, total, acc)

    big, total, acc = state
    return lax.map(one, (query_blocks, big, total, acc))


def student_tile(loop_state, block_entry, student_keys, student_values, score_scale):
    key_gradient, squared_terms = loop_state
    query_portion, target = block_entry
    logit_score = row_scores(query_portion, student_keys) * score_scale
    peak = jnp.max(logit_score, axis=1, keepdims=True)
    weight = jnp.exp(logit_score - peak)
    prob = weight / jnp.sum(weight, axis=1, keepdims=True)
    block_prob = prob.astype(jnp.bfloat16)
    student_output = jnp.dot(block_prob, student_values, preferred_element_type=jnp.float32)
    diff = student_output - target.astype(jnp.float32)
    squared_terms = squared_terms + jnp.sum(diff * diff)
    block_difference = diff.astype(jnp.bfloat16)
    prob_gradient = row_scores(block_difference, student_values)
    inner = jnp.sum(prob * prob_gradient, axis=1, keepdims=True)
    dscore = (prob * (prob_gradient - inner) * score_scale).astype(jnp.bfloat16)
    dkeys = lax.dot_general(
        dscore, query_portion, (((0,), (0,)), ((), ())), preferred_element_type=jnp.float32
    )
    dvals = lax.dot_general(
        block_prob, block_difference, (((0,), (0,)), ((), ())), preferred_element_type=jnp.float32
    )
    key_gradient = key_gradient + jnp.concatenate([dkeys, dvals], axis=1)
    return ((key_gradient, squared_terms), None)


def body(
    queries,
    cache_keys,
    cache_values,
    entry,
    visits,
    doc_length,
    slot_params,
    first_moment,
    second_moment,
):
    shards = lax.axis_size("keys")
    me = lax.axis_index("keys")
    tok, heads, block_width = queries.shape
    rows = tok * heads
    block = math.gcd(rows, 512)
    nblocks = rows // block
    score_scale = 1.0 / math.sqrt(block_width)
    length = doc_length[0]
    query_blocks = queries.reshape(nblocks, block, block_width)
    start = entry[0, 0]
    count = visits[0, 0]
    state = (
        jnp.full((nblocks, block), NEG, jnp.float32),
        jnp.zeros((nblocks, block), jnp.float32),
        jnp.zeros((nblocks, block, block_width), jnp.float32),
    )

    def visit(step, keys, values, loop_state):
        held = jnp.remainder(me - step, shards)
        go = jnp.remainder(-step - start, shards) < count
        return lax.cond(
            go,
            lambda column_index: attend(
                column_index, query_blocks, keys, values, held, length, score_scale
            ),
            lambda column_index: column_index,
            loop_state,
        )

    def turn(step, loop_state):
        keys, values, big, total, acc = loop_state
        big, total, acc = visit(step, keys, values, (big, total, acc))
        keys, values = shifted((keys, values), "keys", 1)
        return (keys, values, big, total, acc)

    keys, values, big, total, acc = lax.fori_loop(
        0, shards - 1, turn, (cache_keys, cache_values) + state
    )
    big, total, acc = visit(shards - 1, keys, values, (big, total, acc))
    teacher_block_list = (acc / total[:, :, None]).astype(jnp.bfloat16)
    teacher_out = teacher_block_list.reshape(tok, heads, block_width)
    copies = slot_params.astype(jnp.bfloat16)
    complete_sum = lax.all_gather(copies, ("keys", "qry"), axis=0, tiled=True)
    student_keys = complete_sum[:, :block_width]
    student_values = complete_sum[:, block_width:]
    initial_state = (jnp.zeros(complete_sum.shape, jnp.float32), jnp.zeros((), jnp.float32))
    (grad_terms, squared_terms), ignored_value = lax.scan(
        lambda column_index, loop_index: student_tile(
            column_index, loop_index, student_keys, student_values, score_scale
        ),
        initial_state,
        (query_blocks, teacher_block_list),
    )
    slot_grad = lax.psum_scatter(grad_terms, ("keys", "qry"), scatter_dimension=0, tiled=True)
    squares_all = lax.psum(squared_terms, ("keys", "qry"))
    loss = (squares_all / (rows * shards * lax.axis_size("qry"))).reshape(1)
    new_first = 0.9 * first_moment + 0.1 * slot_grad
    new_second = 0.95 * second_moment + 0.05 * slot_grad * slot_grad
    new_params = slot_params - 0.02 * new_first / (jnp.sqrt(new_second) + 1e-08)
    return (teacher_out, slot_grad, new_params, new_first, new_second, loss)


def solution(mesh):
    return jax.shard_map(
        body,
        mesh=mesh,
        in_specs=(
            P(("grp", "keys", "qry"), None, None),
            P(("grp", "keys"), None),
            P(("grp", "keys"), None),
            P(("grp", "keys"), "qry"),
            P(("grp", "keys"), "qry"),
            P("grp"),
            P(("grp", "keys", "qry"), None),
            P(("grp", "keys", "qry"), None),
            P(("grp", "keys", "qry"), None),
        ),
        out_specs=(
            P(("grp", "keys", "qry"), None, None),
            P(("grp", "keys", "qry"), None),
            P(("grp", "keys", "qry"), None),
            P(("grp", "keys", "qry"), None),
            P(("grp", "keys", "qry"), None),
            P("grp"),
        ),
        check_vma=False,
    )
```

profile of v0, /device:TPU:0, one launch (start us, length us, event | category | flops | bytes accessed | tf_op | source)
XLA Modules:
  0.0 162.5 jit_solution(8857728833277977669)
XLA Ops:
  8.6 0.8 convert_element_type.42
  9.5 38.7 %all_gather.3 = bf16[1024,256]{1,0:T(8,128)(2,1)S(1)} all-gather(bf16[64,256]{1,0:T(8,128)(2,1)S(1)} %convert_element_type.42), channel_id=1, replica_groups=mesh['grp'=2,'keys'=4,'qry'=4] {'keys','qry'}, dimensions={0}, use_global_device_ids=true | all-gather | bytes 557056 | tf_op jit(solution)/shard_map/all_gather | solution.py:121
  48.3 32.7 %while.82 = (s32[]{:T(128)}, bf16[512,128]{1,0:T(8,128)(2,1)S(1)}, bf16[512,128]{1,0:T(8,128)(2,1)S(1)}, f32[2,512]{1,0:T(2,128)S(1)}, f32[2,512]{1,0:T(2,128)S(...) while((s32[]{:T(128)}, bf16[512,128]{1,0:T(8,128)(2,1)S(1)}, ...), condition=%wide.region_7.8_spmd, body=%wide.region_0.7_spmd.sunk | while | flops 136711200 | bytes 6747030 | solution.py:114
  49.6 1.7 %collective-permute-start.1 = (bf16[512,128]{1,0:T(8,128)(2,1)}, bf16[512,128]{1,0:T(8,128)(2,1)S(1)}, u32[]{:S(2)}, u32[]{:S(2)}) collective-permute-start(bf16[512,128]{1,0:T(8,128)(2,1)} %copy.56), channel_id=1, source_target_pairs={{12,0},{0,4},{4,8},{8,12},{13,1},{1,5},{5,9},{9,13},{14,2},{2,6},{... | collective-permute-start | bytes 393224 | tf_op jit(solution)/shard_map/while/body/eval_jaxpr/ppermute | solution.py:13
  52.6 7.5 %conditional.4 = ((f32[2,512]{1,0:T(2,128)S(1)}, f32[2,512]{1,0:T(2,128)S(1)}, f32[2,512,128]{2,1,0:T(8,128)S(1)})) conditional(s32[]{:T(128)} %convert_element_type.75, (f32[2,512]{1,0:T(2,128)S(1)}, f32[2,512]{1,0:T(2,128)S(1)}, f32[2,512,128]{2,1,0:T(8,128)S(1)}) %tuple.135, (s32[]{:T(128)}, s32[]{:T(128)}, s32[]{:T(128)}, f32[2,512]{1,0:T(2,128)S(1)}, ...), branch_computations={%region_1.1_spmd, %region_2.6_spmd} | conditional | flops 136711184 | bytes 5173698 | solution.py:99
  52.7 7.4 %while.80 = (s32[]{:T(128)}, f32[2,512]{1,0:T(2,128)S(1)}, f32[2,512]{1,0:T(2,128)S(1)}, f32[2,512,128]{2,1,0:T(8,128)S(1)}, f32[2,512]{1,0:T(2,128)S(1)}, /*ind...) while((s32[]{:T(128)}, f32[2,512]{1,0:T(2,128)S(1)}, ...), condition=%wide.region_6.5_spmd.clone, body=%wide.region_3.4_spmd.clone.sunk | while | flops 136711168 | bytes 4108453 | solution.py:40
  52.7 0.7 compare_reduce_fusion.4
  53.4 1.2 fusion.104
  54.6 1.4 fusion.106
  57.1 1.2 fusion.104
  58.3 1.4 fusion.106
  63.4 7.5 %conditional.4 = ((f32[2,512]{1,0:T(2,128)S(1)}, f32[2,512]{1,0:T(2,128)S(1)}, f32[2,512,128]{2,1,0:T(8,128)S(1)})) conditional(s32[]{:T(128)} %convert_element_type.75, (f32[2,512]{1,0:T(2,128)S(1)}, f32[2,512]{1,0:T(2,128)S(1)}, f32[2,512,128]{2,1,0:T(8,128)S(1)}) %tuple.135, (s32[]{:T(128)}, s32[]{:T(128)}, s32[]{:T(128)}, f32[2,512]{1,0:T(2,128)S(1)}, ...), branch_computations={%region_1.1_spmd, %region_2.6_spmd} | conditional | flops 136711184 | bytes 5173698 | solution.py:99
  63.4 7.4 %while.80 = (s32[]{:T(128)}, f32[2,512]{1,0:T(2,128)S(1)}, f32[2,512]{1,0:T(2,128)S(1)}, f32[2,512,128]{2,1,0:T(8,128)S(1)}, f32[2,512]{1,0:T(2,128)S(1)}, /*ind...) while((s32[]{:T(128)}, f32[2,512]{1,0:T(2,128)S(1)}, ...), condition=%wide.region_6.5_spmd.clone, body=%wide.region_3.4_spmd.clone.sunk | while | flops 136711168 | bytes 4108453 | solution.py:40
  64.1 1.2 fusion.104
  65.4 1.4 fusion.106
  67.8 1.2 fusion.104
  69.0 1.4 fusion.106
  73.5 7.5 %conditional.4 = ((f32[2,512]{1,0:T(2,128)S(1)}, f32[2,512]{1,0:T(2,128)S(1)}, f32[2,512,128]{2,1,0:T(8,128)S(1)})) conditional(s32[]{:T(128)} %convert_element_type.75, (f32[2,512]{1,0:T(2,128)S(1)}, f32[2,512]{1,0:T(2,128)S(1)}, f32[2,512,128]{2,1,0:T(8,128)S(1)}) %tuple.135, (s32[]{:T(128)}, s32[]{:T(128)}, s32[]{:T(128)}, f32[2,512]{1,0:T(2,128)S(1)}, ...), branch_computations={%region_1.1_spmd, %region_2.6_spmd} | conditional | flops 136711184 | bytes 5173698 | solution.py:99
  73.6 7.4 %while.80 = (s32[]{:T(128)}, f32[2,512]{1,0:T(2,128)S(1)}, f32[2,512]{1,0:T(2,128)S(1)}, f32[2,512,128]{2,1,0:T(8,128)S(1)}, f32[2,512]{1,0:T(2,128)S(1)}, /*ind...) while((s32[]{:T(128)}, f32[2,512]{1,0:T(2,128)S(1)}, ...), condition=%wide.region_6.5_spmd.clone, body=%wide.region_3.4_spmd.clone.sunk | while | flops 136711168 | bytes 4108453 | solution.py:40
  74.3 1.2 fusion.104
  75.5 1.4 fusion.106
  77.9 1.2 fusion.104
  79.2 1.4 fusion.106
  81.0 3.8 %conditional.2 = ((f32[2,512]{1,0:T(2,128)S(1)}, f32[2,512,128]{2,1,0:T(8,128)S(1)})) conditional(s32[]{:T(128)} %convert_element_type.40, (f32[2,512]{1,0:T(2,128)S(1)}, f32[2,512,128]{2,1,0:T(8,128)S(1)}) %tuple.70, (s32[]{:T(128)}, s32[]{:T(128)}, f32[2,512]{1,0:T(2,128)S(1)}, f32[2,512]{1,0:T(2,128)S(1)}, bf16[2,512,128]{2,1,0:T(8,128)(2,1)S(1)}, ...), branch_computations={%region_8.9_spmd, %region_9.14_spmd} | conditional | flops 136711184 | bytes 5159334 | solution.py:99
  81.1 3.7 %while.81 = (s32[]{:T(128)}, f32[2,512]{1,0:T(2,128)S(1)}, f32[2,512,128]{2,1,0:T(8,128)S(1)}, f32[2,512]{1,0:T(2,128)S(1)}, f32[2,512]{1,0:T(2,128)S(1)}, /*ind...) while((s32[]{:T(128)}, f32[2,512]{1,0:T(2,128)S(1)}, ...), condition=%wide.region_13.13_spmd.clone, body=%wide.region_10.12_spmd.clone.sunk | while | flops 136711168 | bytes 4102297 | solution.py:40
  85.0 10.0 %while.83 = (s32[]{:T(128)}, f32[1024,256]{0,1:T(8,128)S(1)}, f32[]{:T(128)}, bf16[2,512,128]{2,1,0:T(8,128)(2,1)S(1)}, bf16[1024,128]{1,0:T(8,128)(2,1)S(1)}, /...) while((s32[]{:T(128)}, f32[1024,256]{0,1:T(8,128)S(1)}, ...), condition=%wide.region_19.20_spmd.clone, body=%wide.region_14.19_spmd.clone.sunk | while | flops 680589824 | bytes 26753152 | solution.py:125
  86.6 1.1 multiply_reduce_fusion.7
  91.6 1.1 multiply_reduce_fusion.7
  95.1 1.3 copy.15
  96.4 31.9 %psum.7 = f32[]{:T(128)} all-reduce(f32[]{:T(128)} %get-tuple-element.654), channel_id=1, replica_groups=mesh['grp'=2,'keys'=4,'qry'=4] {'keys','qry'}, use_global_device_ids=true, to_apply=%region_21.22 | all-reduce | flops 1 | bytes 8 | tf_op jit(solution)/shard_map/psum | solution.py:133
  129.0 24.0 %reduce-scatter.2.cloned.1.call-done = f32[64,256]{1,0:T(8,128)} async-done(((f32[1024,256]{1,0:T(8,128)}), f32[64,256]{1,0:T(8,128)}) %reduce-scatter.2.cloned.1.call-update) | async-done | bytes 65552 | tf_op jit(solution)/shard_map/reduce_scatter | solution.py:132
  153.0 1.5 divide_subtract_fusion
  (132 shorter events, 20.4 us)
Async XLA Ops:
  7.2 41.1 %copy-start = (bf16[128,8,128]{2,1,0:T(8,128)(2,1)S(1)}, bf16[128,8,128]{2,1,0:T(8,128)(2,1)}, u32[]{:S(2)}) copy-start(bf16[128,8,128]{2,1,0:T(8,128)(2,1)} %param.21) | copy-start | bytes 786436
  7.2 41.1 %copy-start.1 = (bf16[512,128]{1,0:T(8,128)(2,1)S(1)}, bf16[512,128]{1,0:T(8,128)(2,1)}, u32[]{:S(2)}) copy-start(bf16[512,128]{1,0:T(8,128)(2,1)} %param.22) | copy-start | bytes 393220
  7.2 41.1 %copy-start.2 = (bf16[512,128]{1,0:T(8,128)(2,1)S(1)}, bf16[512,128]{1,0:T(8,128)(2,1)}, u32[]{:S(2)}) copy-start(bf16[512,128]{1,0:T(8,128)(2,1)} %param.23) | copy-start | bytes 393220
  7.2 145.8 %reduce-scatter.2.cloned.1.call-start = ((), (), s32[]{:S(2)}) async-start(), calls=%async_computation.1 | async-start | bytes 1114112 | tf_op jit(solution)/shard_map/reduce_scatter | solution.py:132
  49.0 11.1 %collective-permute-start = (bf16[512,128]{1,0:T(8,128)(2,1)}, bf16[512,128]{1,0:T(8,128)(2,1)S(1)}, u32[]{:S(2)}, u32[]{:S(2)}) collective-permute-start(bf16[512,128]{1,0:T(8,128)(2,1)} %copy.55), channel_id=1, source_target_pairs={{12,0},{0,4},{4,8},{8,12},{13,1},{1,5},{5,9},{9,13},{14,2},{2,6},{... | collective-permute-start | bytes 393224 | tf_op jit(solution)/shard_map/while/body/eval_jaxpr/ppermute | solution.py:13
  49.6 10.5 %collective-permute-start.1 = (bf16[512,128]{1,0:T(8,128)(2,1)}, bf16[512,128]{1,0:T(8,128)(2,1)S(1)}, u32[]{:S(2)}, u32[]{:S(2)}) collective-permute-start(bf16[512,128]{1,0:T(8,128)(2,1)} %copy.56), channel_id=1, source_target_pairs={{12,0},{0,4},{4,8},{8,12},{13,1},{1,5},{5,9},{9,13},{14,2},{2,6},{... | collective-permute-start | bytes 393224 | tf_op jit(solution)/shard_map/while/body/eval_jaxpr/ppermute | solution.py:13
  60.8 10.0 %collective-permute-start = (bf16[512,128]{1,0:T(8,128)(2,1)}, bf16[512,128]{1,0:T(8,128)(2,1)S(1)}, u32[]{:S(2)}, u32[]{:S(2)}) collective-permute-start(bf16[512,128]{1,0:T(8,128)(2,1)} %copy.55), channel_id=1, source_target_pairs={{12,0},{0,4},{4,8},{8,12},{13,1},{1,5},{5,9},{9,13},{14,2},{2,6},{... | collective-permute-start | bytes 393224 | tf_op jit(solution)/shard_map/while/body/eval_jaxpr/ppermute | solution.py:13
  61.5 9.4 %collective-permute-start.1 = (bf16[512,128]{1,0:T(8,128)(2,1)}, bf16[512,128]{1,0:T(8,128)(2,1)S(1)}, u32[]{:S(2)}, u32[]{:S(2)}) collective-permute-start(bf16[512,128]{1,0:T(8,128)(2,1)} %copy.56), channel_id=1, source_target_pairs={{12,0},{0,4},{4,8},{8,12},{13,1},{1,5},{5,9},{9,13},{14,2},{2,6},{... | collective-permute-start | bytes 393224 | tf_op jit(solution)/shard_map/while/body/eval_jaxpr/ppermute | solution.py:13
  71.5 9.5 %collective-permute-start = (bf16[512,128]{1,0:T(8,128)(2,1)}, bf16[512,128]{1,0:T(8,128)(2,1)S(1)}, u32[]{:S(2)}, u32[]{:S(2)}) collective-permute-start(bf16[512,128]{1,0:T(8,128)(2,1)} %copy.55), channel_id=1, source_target_pairs={{12,0},{0,4},{4,8},{8,12},{13,1},{1,5},{5,9},{9,13},{14,2},{2,6},{... | collective-permute-start | bytes 393224 | tf_op jit(solution)/shard_map/while/body/eval_jaxpr/ppermute | solution.py:13
  72.2 8.8 %collective-permute-start.1 = (bf16[512,128]{1,0:T(8,128)(2,1)}, bf16[512,128]{1,0:T(8,128)(2,1)S(1)}, u32[]{:S(2)}, u32[]{:S(2)}) collective-permute-start(bf16[512,128]{1,0:T(8,128)(2,1)} %copy.56), channel_id=1, source_target_pairs={{12,0},{0,4},{4,8},{8,12},{13,1},{1,5},{5,9},{9,13},{14,2},{2,6},{... | collective-permute-start | bytes 393224 | tf_op jit(solution)/shard_map/while/body/eval_jaxpr/ppermute | solution.py:13
  95.0 59.5 %copy-start.3 = (bf16[2,512,128]{2,1,0:T(8,128)(2,1)}, bf16[2,512,128]{2,1,0:T(8,128)(2,1)S(1)}, u32[]{:S(2)}) copy-start(bf16[2,512,128]{2,1,0:T(8,128)(2,1)S(1)} %get-tuple-element.1306) | copy-start | bytes 786436
  95.0 58.0 %copy-start.4 = (f32[64,256]{1,0:T(8,128)S(1)}, f32[64,256]{1,0:T(8,128)}, u32[]{:S(2)}) copy-start(f32[64,256]{1,0:T(8,128)} %param.27) | copy-start | bytes 196612
  95.0 57.9 %copy-start.5 = (f32[64,256]{1,0:T(8,128)S(1)}, f32[64,256]{1,0:T(8,128)}, u32[]{:S(2)}) copy-start(f32[64,256]{1,0:T(8,128)} %param.28) | copy-start | bytes 196612
  95.1 57.9 %copy-start.6 = (f32[64,256]{1,0:T(8,128)S(1)}, f32[64,256]{1,0:T(8,128)}, u32[]{:S(2)}) copy-start(f32[64,256]{1,0:T(8,128)} %param.29) | copy-start | bytes 196612
Sparse Core Ops, SparseCore 0:
  96.5 56.4 reduce-scatter.1
where the time goes:
time: 163 us
  blocking collectives  70.6 us (43%)
  waiting for transfers between devices  24.1 us (15%)
  matrix products  23.3 us (14%)
  between operations  17.3 us (11%)
  other arithmetic  12.6 us (8%)
  loops' own time  6.18 us (4%)
  local copies, waits for them, and re-layouts  6.17 us (4%)
  starting transfers between devices  2.3 us (1%)
    all_gather x1, blocking collectives, body(): complete_sum = lax.all_gather(copies, ('keys', 'qry'), axis=0, tiled=True)  38.7 us
    psum x1, blocking collectives, body(): squares_all = lax.psum(squared_terms, ('keys', 'qry'))  31.9 us
    reduce_scatter x1, waiting for transfers between devices, body(): lax.psum_scatter(grad_terms, ('keys', 'qry'), scatter_dimension=0, tiled=...  24 us
    dot_general x12, matrix products, row_scores(): lax.dot_general(left, right, (((1,), (1,)), ((), ())), preferred_element_...  10.1 us
    dot_general x8, matrix products, one(): jnp.dot(weight.astype(jnp.bfloat16), values, preferred_element_type=jnp.f...  9.39 us
    lt x8, other arithmetic, attend(): live = (place < length)[None, :]  5.37 us
    another operation x1, loops' own time, body(): lax.fori_loop(0, shards - 1, turn, (cache_keys, cache_values) + state)  4.07 us
    another operation x8, local copies, waits for them, and re-layouts  3.92 us
  transfers between devices with their start and end apart: 7, of which 1 were waited for; matrix products, arithmetic and copies ran while one was open for 15% of the time, Pallas kernels for 0%

commit v1 on v0

--- a/solution.py
+++ b/solution.py
@@ -130,7 +130,8 @@
         (query_blocks, teacher_block_list),
     )
     slot_grad = lax.psum_scatter(grad_terms, ("keys", "qry"), scatter_dimension=0, tiled=True)
-    squares_all = lax.psum(squared_terms, ("keys", "qry"))
+    parts = lax.all_gather(squared_terms, ("keys", "qry"), axis=0, tiled=False)
+    squares_all = parts.sum(axis=0)
     loss = (squares_all / (rows * shards * lax.axis_size("qry"))).reshape(1)
     new_first = 0.9 * first_moment + 0.1 * slot_grad
     new_second = 0.95 * second_moment + 0.05 * slot_grad * slot_grad

time: 163 us -> 163 us (level)
    psum x1 -> x0, blocking collectives: 31.9 us -> none  [body(): squares_all = lax.psum(squared_terms, ('keys', 'qry'))]
    unnamed x0 -> x1, blocking collectives: none -> 30.9 us
  transfers between devices with their start and end apart: 7 -> 7, of which waited for: 1 -> 1; matrix products, arithmetic and copies ran while one was open for 15% -> 16% of each run, Pallas kernels for 0% -> 0%
where the time goes in v1:
time: 163 us
  blocking collectives  69.6 us (43%)
  matrix products  23.3 us (14%)
  waiting for transfers between devices  23.2 us (14%)
  between operations  17.4 us (11%)
  other arithmetic  13.2 us (8%)
  local copies, waits for them, and re-layouts  7.52 us (5%)
  loops' own time  6.18 us (4%)
  starting transfers between devices  2.3 us (1%)
    all_gather x1, blocking collectives, body(): complete_sum = lax.all_gather(copies, ('keys', 'qry'), axis=0, tiled=True)  38.7 us
    unnamed x1, blocking collectives  30.9 us
    reduce_scatter x1, waiting for transfers between devices, body(): lax.psum_scatter(grad_terms, ('keys', 'qry'), scatter_dimension=0, tiled=...  23.2 us
    dot_general x12, matrix products, row_scores(): lax.dot_general(left, right, (((1,), (1,)), ((), ())), preferred_element_...  10.1 us
    dot_general x8, matrix products, one(): jnp.dot(weight.astype(jnp.bfloat16), values, preferred_element_type=jnp.f...  9.39 us
    lt x8, other arithmetic, attend(): live = (place < length)[None, :]  5.37 us
    another operation x1, loops' own time, body(): lax.fori_loop(0, shards - 1, turn, (cache_keys, cache_values) + state)  4.07 us
    another operation x8, local copies, waits for them, and re-layouts  3.92 us
  transfers between devices with their start and end apart: 7, of which 1 were waited for; matrix products, arithmetic and copies ran while one was open for 16% of the time, Pallas kernels for 0%

profile of v1, /device:TPU:0, one launch (start us, length us, event | category | flops | bytes accessed | tf_op | source)
XLA Modules:
  0.0 162.6 jit_solution(17164529904798180038)
XLA Ops:
  8.6 0.8 convert_element_type.42
  9.5 38.7 %all_gather.9 = bf16[1024,256]{1,0:T(8,128)(2,1)S(1)} all-gather(bf16[64,256]{1,0:T(8,128)(2,1)S(1)} %convert_element_type.42), channel_id=1, replica_groups=mesh['grp'=2,'keys'=4,'qry'=4] {'keys','qry'}, dimensions={0}, use_global_device_ids=true | all-gather | bytes 557056 | tf_op jit(solution)/shard_map/all_gather | solution.py:121
  48.3 32.7 %while.82 = (s32[]{:T(128)}, bf16[512,128]{1,0:T(8,128)(2,1)S(1)}, bf16[512,128]{1,0:T(8,128)(2,1)S(1)}, f32[2,512]{1,0:T(2,128)S(1)}, f32[2,512]{1,0:T(2,128)S(...) while((s32[]{:T(128)}, bf16[512,128]{1,0:T(8,128)(2,1)S(1)}, ...), condition=%wide.region_7.8_spmd, body=%wide.region_0.7_spmd.sunk | while | flops 136711200 | bytes 6747030 | solution.py:114
  49.6 1.7 %collective-permute-start.1 = (bf16[512,128]{1,0:T(8,128)(2,1)}, bf16[512,128]{1,0:T(8,128)(2,1)S(1)}, u32[]{:S(2)}, u32[]{:S(2)}) collective-permute-start(bf16[512,128]{1,0:T(8,128)(2,1)} %copy.56), channel_id=1, source_target_pairs={{12,0},{0,4},{4,8},{8,12},{13,1},{1,5},{5,9},{9,13},{14,2},{2,6},{... | collective-permute-start | bytes 393224 | tf_op jit(solution)/shard_map/while/body/eval_jaxpr/ppermute | solution.py:13
  52.6 7.5 %conditional.4 = ((f32[2,512]{1,0:T(2,128)S(1)}, f32[2,512]{1,0:T(2,128)S(1)}, f32[2,512,128]{2,1,0:T(8,128)S(1)})) conditional(s32[]{:T(128)} %convert_element_type.75, (f32[2,512]{1,0:T(2,128)S(1)}, f32[2,512]{1,0:T(2,128)S(1)}, f32[2,512,128]{2,1,0:T(8,128)S(1)}) %tuple.135, (s32[]{:T(128)}, s32[]{:T(128)}, s32[]{:T(128)}, f32[2,512]{1,0:T(2,128)S(1)}, ...), branch_computations={%region_1.1_spmd, %region_2.6_spmd} | conditional | flops 136711184 | bytes 5173698 | solution.py:99
  52.7 7.4 %while.80 = (s32[]{:T(128)}, f32[2,512]{1,0:T(2,128)S(1)}, f32[2,512]{1,0:T(2,128)S(1)}, f32[2,512,128]{2,1,0:T(8,128)S(1)}, f32[2,512]{1,0:T(2,128)S(1)}, /*ind...) while((s32[]{:T(128)}, f32[2,512]{1,0:T(2,128)S(1)}, ...), condition=%wide.region_6.5_spmd.clone, body=%wide.region_3.4_spmd.clone.sunk | while | flops 136711168 | bytes 4108453 | solution.py:40
  53.4 1.2 fusion.104
  54.6 1.4 fusion.106
  57.1 1.2 fusion.104
  58.3 1.4 fusion.106
  63.4 7.5 %conditional.4 = ((f32[2,512]{1,0:T(2,128)S(1)}, f32[2,512]{1,0:T(2,128)S(1)}, f32[2,512,128]{2,1,0:T(8,128)S(1)})) conditional(s32[]{:T(128)} %convert_element_type.75, (f32[2,512]{1,0:T(2,128)S(1)}, f32[2,512]{1,0:T(2,128)S(1)}, f32[2,512,128]{2,1,0:T(8,128)S(1)}) %tuple.135, (s32[]{:T(128)}, s32[]{:T(128)}, s32[]{:T(128)}, f32[2,512]{1,0:T(2,128)S(1)}, ...), branch_computations={%region_1.1_spmd, %region_2.6_spmd} | conditional | flops 136711184 | bytes 5173698 | solution.py:99
  63.4 7.4 %while.80 = (s32[]{:T(128)}, f32[2,512]{1,0:T(2,128)S(1)}, f32[2,512]{1,0:T(2,128)S(1)}, f32[2,512,128]{2,1,0:T(8,128)S(1)}, f32[2,512]{1,0:T(2,128)S(1)}, /*ind...) while((s32[]{:T(128)}, f32[2,512]{1,0:T(2,128)S(1)}, ...), condition=%wide.region_6.5_spmd.clone, body=%wide.region_3.4_spmd.clone.sunk | while | flops 136711168 | bytes 4108453 | solution.py:40
  64.1 1.2 fusion.104
  65.4 1.4 fusion.106
  67.8 1.2 fusion.104
  69.0 1.4 fusion.106
  73.5 7.5 %conditional.4 = ((f32[2,512]{1,0:T(2,128)S(1)}, f32[2,512]{1,0:T(2,128)S(1)}, f32[2,512,128]{2,1,0:T(8,128)S(1)})) conditional(s32[]{:T(128)} %convert_element_type.75, (f32[2,512]{1,0:T(2,128)S(1)}, f32[2,512]{1,0:T(2,128)S(1)}, f32[2,512,128]{2,1,0:T(8,128)S(1)}) %tuple.135, (s32[]{:T(128)}, s32[]{:T(128)}, s32[]{:T(128)}, f32[2,512]{1,0:T(2,128)S(1)}, ...), branch_computations={%region_1.1_spmd, %region_2.6_spmd} | conditional | flops 136711184 | bytes 5173698 | solution.py:99
  73.6 7.4 %while.80 = (s32[]{:T(128)}, f32[2,512]{1,0:T(2,128)S(1)}, f32[2,512]{1,0:T(2,128)S(1)}, f32[2,512,128]{2,1,0:T(8,128)S(1)}, f32[2,512]{1,0:T(2,128)S(1)}, /*ind...) while((s32[]{:T(128)}, f32[2,512]{1,0:T(2,128)S(1)}, ...), condition=%wide.region_6.5_spmd.clone, body=%wide.region_3.4_spmd.clone.sunk | while | flops 136711168 | bytes 4108453 | solution.py:40
  74.3 1.2 fusion.104
  75.5 1.4 fusion.106
  77.9 1.2 fusion.104
  79.2 1.4 fusion.106
  81.0 3.8 %conditional.2 = ((f32[2,512]{1,0:T(2,128)S(1)}, f32[2,512,128]{2,1,0:T(8,128)S(1)})) conditional(s32[]{:T(128)} %convert_element_type.40, (f32[2,512]{1,0:T(2,128)S(1)}, f32[2,512,128]{2,1,0:T(8,128)S(1)}) %tuple.70, (s32[]{:T(128)}, s32[]{:T(128)}, f32[2,512]{1,0:T(2,128)S(1)}, f32[2,512]{1,0:T(2,128)S(1)}, bf16[2,512,128]{2,1,0:T(8,128)(2,1)S(1)}, ...), branch_computations={%region_8.9_spmd, %region_9.14_spmd} | conditional | flops 136711184 | bytes 5159334 | solution.py:99
  81.1 3.7 %while.81 = (s32[]{:T(128)}, f32[2,512]{1,0:T(2,128)S(1)}, f32[2,512,128]{2,1,0:T(8,128)S(1)}, f32[2,512]{1,0:T(2,128)S(1)}, f32[2,512]{1,0:T(2,128)S(1)}, /*ind...) while((s32[]{:T(128)}, f32[2,512]{1,0:T(2,128)S(1)}, ...), condition=%wide.region_13.13_spmd.clone, body=%wide.region_10.12_spmd.clone.sunk | while | flops 136711168 | bytes 4102297 | solution.py:40
  85.0 10.0 %while.83 = (s32[]{:T(128)}, f32[1024,256]{0,1:T(8,128)S(1)}, f32[]{:T(128)}, bf16[2,512,128]{2,1,0:T(8,128)(2,1)S(1)}, bf16[1024,128]{1,0:T(8,128)(2,1)S(1)}, /...) while((s32[]{:T(128)}, f32[1024,256]{0,1:T(8,128)S(1)}, ...), condition=%wide.region_19.20_spmd.clone, body=%wide.region_14.19_spmd.clone.sunk | while | flops 680589824 | bytes 26753152 | solution.py:125
  86.6 1.1 multiply_reduce_fusion.7
  91.6 1.1 multiply_reduce_fusion.7
  95.1 1.3 copy.15
  97.0 0.8 dynamic-update-slice
  97.8 30.9 %all-reduce = f32[16]{0:T(128)S(1)} all-reduce(f32[16]{0:T(128)S(1)} %dynamic-update-slice), channel_id=1, replica_groups=mesh['grp'=2,'keys'=4,'qry'=4] {'keys','qry'}, use_global_device_ids=true, to_apply=%add | all-reduce | flops 16 | bytes 128
  129.9 23.2 %reduce-scatter.2.cloned.1.call-done = f32[64,256]{1,0:T(8,128)} async-done(((f32[1024,256]{1,0:T(8,128)}), f32[64,256]{1,0:T(8,128)}) %reduce-scatter.2.cloned.1.call-update) | async-done | bytes 65552 | tf_op jit(solution)/shard_map/reduce_scatter | solution.py:132
  153.1 1.5 divide_subtract_fusion
  (138 shorter events, 22.3 us)
Async XLA Ops:
  7.2 41.1 %copy-start = (bf16[128,8,128]{2,1,0:T(8,128)(2,1)S(1)}, bf16[128,8,128]{2,1,0:T(8,128)(2,1)}, u32[]{:S(2)}) copy-start(bf16[128,8,128]{2,1,0:T(8,128)(2,1)} %param.21) | copy-start | bytes 786436
  7.2 41.1 %copy-start.1 = (bf16[512,128]{1,0:T(8,128)(2,1)S(1)}, bf16[512,128]{1,0:T(8,128)(2,1)}, u32[]{:S(2)}) copy-start(bf16[512,128]{1,0:T(8,128)(2,1)} %param.22) | copy-start | bytes 393220
  7.2 41.1 %copy-start.2 = (bf16[512,128]{1,0:T(8,128)(2,1)S(1)}, bf16[512,128]{1,0:T(8,128)(2,1)}, u32[]{:S(2)}) copy-start(bf16[512,128]{1,0:T(8,128)(2,1)} %param.23) | copy-start | bytes 393220
  7.2 145.9 %reduce-scatter.2.cloned.1.call-start = ((), (), s32[]{:S(2)}) async-start(), calls=%async_computation.1 | async-start | bytes 1114112 | tf_op jit(solution)/shard_map/reduce_scatter | solution.py:132
  49.0 11.1 %collective-permute-start = (bf16[512,128]{1,0:T(8,128)(2,1)}, bf16[512,128]{1,0:T(8,128)(2,1)S(1)}, u32[]{:S(2)}, u32[]{:S(2)}) collective-permute-start(bf16[512,128]{1,0:T(8,128)(2,1)} %copy.55), channel_id=1, source_target_pairs={{12,0},{0,4},{4,8},{8,12},{13,1},{1,5},{5,9},{9,13},{14,2},{2,6},{... | collective-permute-start | bytes 393224 | tf_op jit(solution)/shard_map/while/body/eval_jaxpr/ppermute | solution.py:13
  49.6 10.5 %collective-permute-start.1 = (bf16[512,128]{1,0:T(8,128)(2,1)}, bf16[512,128]{1,0:T(8,128)(2,1)S(1)}, u32[]{:S(2)}, u32[]{:S(2)}) collective-permute-start(bf16[512,128]{1,0:T(8,128)(2,1)} %copy.56), channel_id=1, source_target_pairs={{12,0},{0,4},{4,8},{8,12},{13,1},{1,5},{5,9},{9,13},{14,2},{2,6},{... | collective-permute-start | bytes 393224 | tf_op jit(solution)/shard_map/while/body/eval_jaxpr/ppermute | solution.py:13
  60.8 10.0 %collective-permute-start = (bf16[512,128]{1,0:T(8,128)(2,1)}, bf16[512,128]{1,0:T(8,128)(2,1)S(1)}, u32[]{:S(2)}, u32[]{:S(2)}) collective-permute-start(bf16[512,128]{1,0:T(8,128)(2,1)} %copy.55), channel_id=1, source_target_pairs={{12,0},{0,4},{4,8},{8,12},{13,1},{1,5},{5,9},{9,13},{14,2},{2,6},{... | collective-permute-start | bytes 393224 | tf_op jit(solution)/shard_map/while/body/eval_jaxpr/ppermute | solution.py:13
  61.5 9.4 %collective-permute-start.1 = (bf16[512,128]{1,0:T(8,128)(2,1)}, bf16[512,128]{1,0:T(8,128)(2,1)S(1)}, u32[]{:S(2)}, u32[]{:S(2)}) collective-permute-start(bf16[512,128]{1,0:T(8,128)(2,1)} %copy.56), channel_id=1, source_target_pairs={{12,0},{0,4},{4,8},{8,12},{13,1},{1,5},{5,9},{9,13},{14,2},{2,6},{... | collective-permute-start | bytes 393224 | tf_op jit(solution)/shard_map/while/body/eval_jaxpr/ppermute | solution.py:13
  71.5 9.5 %collective-permute-start = (bf16[512,128]{1,0:T(8,128)(2,1)}, bf16[512,128]{1,0:T(8,128)(2,1)S(1)}, u32[]{:S(2)}, u32[]{:S(2)}) collective-permute-start(bf16[512,128]{1,0:T(8,128)(2,1)} %copy.55), channel_id=1, source_target_pairs={{12,0},{0,4},{4,8},{8,12},{13,1},{1,5},{5,9},{9,13},{14,2},{2,6},{... | collective-permute-start | bytes 393224 | tf_op jit(solution)/shard_map/while/body/eval_jaxpr/ppermute | solution.py:13
  72.2 8.8 %collective-permute-start.1 = (bf16[512,128]{1,0:T(8,128)(2,1)}, bf16[512,128]{1,0:T(8,128)(2,1)S(1)}, u32[]{:S(2)}, u32[]{:S(2)}) collective-permute-start(bf16[512,128]{1,0:T(8,128)(2,1)} %copy.56), channel_id=1, source_target_pairs={{12,0},{0,4},{4,8},{8,12},{13,1},{1,5},{5,9},{9,13},{14,2},{2,6},{... | collective-permute-start | bytes 393224 | tf_op jit(solution)/shard_map/while/body/eval_jaxpr/ppermute | solution.py:13
  95.0 59.6 %copy-start.3 = (bf16[2,512,128]{2,1,0:T(8,128)(2,1)}, bf16[2,512,128]{2,1,0:T(8,128)(2,1)S(1)}, u32[]{:S(2)}) copy-start(bf16[2,512,128]{2,1,0:T(8,128)(2,1)S(1)} %get-tuple-element.1306) | copy-start | bytes 786436
  95.0 1.4 copy-start.7
  95.0 58.0 %copy-start.4 = (f32[64,256]{1,0:T(8,128)S(1)}, f32[64,256]{1,0:T(8,128)}, u32[]{:S(2)}) copy-start(f32[64,256]{1,0:T(8,128)} %param.27) | copy-start | bytes 196612
  95.1 58.0 %copy-start.5 = (f32[64,256]{1,0:T(8,128)S(1)}, f32[64,256]{1,0:T(8,128)}, u32[]{:S(2)}) copy-start(f32[64,256]{1,0:T(8,128)} %param.28) | copy-start | bytes 196612
  95.1 58.0 %copy-start.6 = (f32[64,256]{1,0:T(8,128)S(1)}, f32[64,256]{1,0:T(8,128)}, u32[]{:S(2)}) copy-start(f32[64,256]{1,0:T(8,128)} %param.29) | copy-start | bytes 196612
Sparse Core Ops, SparseCore 0:
  96.6 56.4 reduce-scatter.1
